TPU v7x, 32 devices: a whole 2x2x4 slice. The times are simulated.
32 devices in a mesh: rep: 2 (over y), tp: 4 (over z), fs: 4 (over x, core).
Axes of the slice: x: 2, y: 2, z: 4, core: 2. Of those that a mesh axis runs over, the one named last changes fastest.
Arguments:
- hidden: bfloat16 [16, 8192], P(('rep', 'fs'), 'tp'), may hold values from -6 to 6
- cache_key: bfloat16 [16, 2048, 1024], P(('rep', 'fs'), None, 'tp'), may hold values from -1300 to 1300
- cache_value: bfloat16 [16, 2048, 1024], P(('rep', 'fs'), None, 'tp'), may hold values from -6 to 6
- lengths: int32 [16], P(('rep', 'fs')), may hold values from 8 to 2047
- owner: int32 [1], replicated, may hold values from 0 to 8191
- query_weight: bfloat16 [2, 8192, 4096], P('rep', 'fs', 'tp'), may hold values from -0.0625 to 0.0625
- key_weight: bfloat16 [2, 8192, 1024], P('rep', 'fs', 'tp'), may hold values from -0.0625 to 0.0625
- value_weight: bfloat16 [2, 8192, 1024], P('rep', 'fs', 'tp'), may hold values from -0.0625 to 0.0625
- out_weight: bfloat16 [2, 4096, 8192], P('rep', 'tp', 'fs'), may hold values from -0.09375 to 0.09375
Outputs:
- mixed: bfloat16 [16, 8192], P(('rep', 'fs'), 'tp')
- new_key: bfloat16 [16, 1024], P(('rep', 'fs'), 'tp')
- new_value: bfloat16 [16, 1024], P(('rep', 'fs'), 'tp')
- fresh_query: bfloat16 [2, 8192, 4096], P('rep', 'fs', 'tp')
- fresh_key: bfloat16 [2, 8192, 1024], P('rep', 'fs', 'tp')
- fresh_value: bfloat16 [2, 8192, 1024], P('rep', 'fs', 'tp')
- fresh_out: bfloat16 [2, 4096, 8192], P('rep', 'tp', 'fs')
Inputs may be any that keep to these rules, and one draw needn't show every extreme that they name: `lengths`: the number of positions already in each sequence's cache; the new token stands at that position.
All inputs are finite; a program needn't handle non-finite values.
Results may differ from a plain program's by a relative error of at most 0.0065.
Values may be sent and summed in bfloat16 or wider, within the bound.
A program may use at most 64 MiB of HBM per device.

v0:
```python
import jax
import jax.numpy as jnp
from jax import lax
from jax.sharding import PartitionSpec as P

DH = 128


rope_base = 500000.0
epsilon = 1e-05


def exchange(shard, axis, root):
    size = lax.axis_size(axis)
    rank = lax.axis_index(axis)
    if size & (size - 1):
        return lax.psum(jnp.where(rank == root, shard, jnp.zeros_like(shard)), axis)
    away = jnp.bitwise_xor(rank, root)
    step = 1
    while step < size:
        pairs = [(i, i ^ step) for i in range(size)]
        received = lax.ppermute(shard, axis, pairs)
        takes = (away >= step) & (away < 2 * step)
        shard = jnp.where(takes, received, shard)
        step *= 2
    return shard


OUT_CUTS = (0, 3, 6, 8)


def gather(shard, axis, dim):
    size = lax.axis_size(axis)
    copies = jnp.broadcast_to(shard[None], (size,) + shard.shape)
    pieces = lax.all_to_all(copies, axis, split_axis=0, concat_axis=0, tiled=True)
    return jnp.concatenate([pieces[i] for i in range(size)], axis=dim)


def scatter_sum(terms, axis):
    return jnp.sum(lax.all_to_all(terms, axis, split_axis=0, concat_axis=0, tiled=True), axis=0)


def rotate(heads, positions):
    half_dim = heads.shape[-1] // 2
    frequency = rope_base ** (-(jnp.arange(half_dim, dtype=jnp.float32) * 2.0 / heads.shape[-1]))
    angles = positions.astype(jnp.float32)[:, None] * frequency[None, :]
    cosine = jnp.cos(angles)[:, None, :]
    sine_part = jnp.sin(angles)[:, None, :]
    first_half = heads[..., :half_dim]
    second_half = heads[..., half_dim:]
    return jnp.concatenate(
        [
            first_half * cosine - second_half * sine_part,
            second_half * cosine + first_half * sine_part,
        ],
        axis=-1,
    )


def attend(query, own_key, own_value, cache_key, cache_value, lengths):
    seqs, span, _ = cache_key.shape
    kv_local = query.shape[1]
    head_size = query.shape[3]
    keys_view = cache_key.reshape(seqs, span, kv_local, head_size)
    values_view = cache_value.reshape(seqs, span, kv_local, head_size)
    scale = head_size ** (-0.5)
    scores = (
        jnp.einsum("shgd,sthd->shgt", query, keys_view, preferred_element_type=jnp.float32) * scale
    )
    own_score = (
        jnp.einsum("shgd,shd->shg", query, own_key, preferred_element_type=jnp.float32) * scale
    )
    live = (jnp.arange(span, dtype=jnp.int32)[None, :] < lengths[:, None])[:, None, None, :]
    masked = jnp.where(live, scores, -jnp.inf)
    row_max = jnp.maximum(jnp.max(masked, axis=-1), own_score)
    weights = jnp.where(live, jnp.exp(scores - row_max[..., None]), 0.0)
    own_weight = jnp.exp(own_score - row_max)
    denominator = jnp.sum(weights, axis=-1) + own_weight
    probs = (weights / denominator[..., None]).astype(jnp.bfloat16)
    own_prob = (own_weight / denominator).astype(jnp.bfloat16)
    context = jnp.einsum("shgt,sthd->shgd", probs, values_view, preferred_element_type=jnp.float32)
    return (
        context
        + own_prob.astype(jnp.float32)[..., None] * own_value.astype(jnp.float32)[:, :, None, :]
    )


def local(
    hidden,
    cache_key,
    cache_value,
    lengths,
    owner,
    query_weight,
    key_weight,
    value_weight,
    out_weight,
):
    owner_rank = owner[0] % lax.axis_size("rep")
    features = gather(hidden, "tp", 1)
    hidden_wide = features.astype(jnp.float32)
    normed = (
        hidden_wide
        * lax.rsqrt(jnp.mean(hidden_wide * hidden_wide, axis=-1, keepdims=True) + epsilon)
    ).astype(jnp.bfloat16)
    fresh_key = exchange(key_weight, "rep", owner_rank)
    fresh_value = exchange(value_weight, "rep", owner_rank)
    fresh_query = exchange(query_weight, "rep", owner_rank)
    edges = [out_weight.shape[1] * cut // 8 for cut in OUT_CUTS]
    spans = list(zip(edges[:-1], edges[1:]))
    out_pieces = [exchange(out_weight[:, low:high], "rep", owner_rank) for low, high in spans]
    fresh_out = out_weight
    for (low, high), piece in zip(spans, out_pieces):
        fresh_out = lax.dynamic_update_slice(fresh_out, piece, (0, low, 0))
    query_rows = fresh_query[0]
    key_rows = fresh_key[0]
    value_rows = fresh_value[0]
    seqs = normed.shape[0]
    query_width = query_rows.shape[1]
    key_width = key_rows.shape[1]
    token_block = lax.all_to_all(normed, "fs", split_axis=1, concat_axis=0, tiled=True)
    groups = lax.axis_size("fs")
    joined = scatter_sum(
        jnp.concatenate(
            [
                jnp.dot(token_block, query_rows, preferred_element_type=jnp.float32),
                jnp.dot(token_block, key_rows, preferred_element_type=jnp.float32),
                jnp.dot(token_block, value_rows, preferred_element_type=jnp.float32),
            ],
            axis=1,
        ).reshape(groups, seqs, query_width + 2 * key_width),
        "fs",
    )
    query_proj = joined[:, :query_width]
    key_proj = joined[:, query_width : query_width + key_width]
    value_proj = joined[:, query_width + key_width :]
    q_heads = query_proj.shape[1] // DH
    kv_heads = key_proj.shape[1] // DH
    query_rot = rotate(query_proj.reshape(seqs, q_heads, DH), lengths).astype(jnp.bfloat16)
    query_rot = query_rot.reshape(seqs, kv_heads, q_heads // kv_heads, DH)
    key_new = rotate(key_proj.reshape(seqs, kv_heads, DH), lengths).astype(jnp.bfloat16)
    value_new = value_proj.astype(jnp.bfloat16).reshape(seqs, kv_heads, DH)
    context = attend(query_rot, key_new, value_new, cache_key, cache_value, lengths)
    context = context.astype(jnp.bfloat16).reshape(seqs, q_heads * DH)
    group_context = gather(context, "fs", 0)
    partial_out = 0.0
    for (low, high), piece in zip(spans, out_pieces):
        partial_out = partial_out + jnp.dot(
            group_context[:, low:high],
            piece[0],
            preferred_element_type=jnp.float32,
        )
    terms = lax.all_to_all(partial_out, "fs", split_axis=0, concat_axis=1, tiled=True)
    model_groups = lax.axis_size("tp")
    terms = terms.reshape(seqs, model_groups, -1).transpose(1, 0, 2)
    summed = scatter_sum(terms, "tp")
    mixed = (summed + hidden.astype(jnp.float32)).astype(jnp.bfloat16)
    return (
        mixed,
        key_new.reshape(seqs, kv_heads * DH),
        value_new.reshape(seqs, kv_heads * DH),
        fresh_query,
        fresh_key,
        fresh_value,
        fresh_out,
    )


def solution(mesh):
    return jax.shard_map(
        local,
        mesh=mesh,
        in_specs=(
            P(("rep", "fs"), "tp"),
            P(("rep", "fs"), None, "tp"),
            P(("rep", "fs"), None, "tp"),
            P(("rep", "fs")),
            P(),
            P("rep", "fs", "tp"),
            P("rep", "fs", "tp"),
            P("rep", "fs", "tp"),
            P("rep", "tp", "fs"),
        ),
        out_specs=(
            P(("rep", "fs"), "tp"),
            P(("rep", "fs"), "tp"),
            P(("rep", "fs"), "tp"),
            P("rep", "fs", "tp"),
            P("rep", "fs", "tp"),
            P("rep", "fs", "tp"),
            P("rep", "tp", "fs"),
        ),
        check_vma=False,
    )
```

profile of v0, /device:TPU:0, one launch (start us, length us, event | category | flops | bytes accessed | tf_op | source)
XLA Modules:
  0.0 278.4 jit_solution(3690747553470232116)
XLA Ops:
  0.6 0.0 copy-start
  0.7 3.1 %collective-permute-start = (bf16[1,2048,1024]{2,1,0:T(8,128)(2,1)}, bf16[1,2048,1024]{2,1,0:T(8,128)(2,1)}, u32[]{:S(2)}, u32[]{:S(2)}) collective-permute-start(bf16[1,2048,1024]{2,1,0:T(8,128)(2,1)} %param.14), channel_id=1, source_target_pairs={{0,16},{16,0},{1,17},{17,1},{2,18},{18,2},{3,19},{19,3},{4,20},{20... | collective-permute-start | bytes 12582920 | tf_op jit(solution)/shard_map/ppermute | solution.py:22
  3.7 2.8 slice.80
  6.5 0.2 collective-permute-start.3
  6.7 2.4 slice.84
  9.1 1.9 collective-permute-start.5
  10.9 0.6 broadcast_in_dim.25
  11.6 4.9 %all-to-all-start = ((bf16[4,2,2048]{2,1,0:T(2,128)(2,1)}), bf16[4,2,2048]{2,1,0:T(2,128)(2,1)S(1)}, u32[]{:S(2)}, u32[]{:S(2)}) async-start(bf16[4,2,2048]{2,1,0:T(2,128)(2,1)} %broadcast_in_dim.25), calls=%async_computation | async-start | bytes 65536 | tf_op jit(solution)/shard_map/all_to_all | solution.py:35
  16.4 0.5 collective-permute-start.2
  16.9 1.5 collective-permute-start.1
  18.5 0.1 iota_compare_fusion
  18.6 3.5 %all-to-all-done = bf16[4,2,2048]{2,1,0:T(2,128)(2,1)S(1)} async-done(((bf16[4,2,2048]{2,1,0:T(2,128)(2,1)}), bf16[4,2,2048]{2,1,0:T(2,128)(2,1)S(1)}, u32[]{:S(2)}, u32[]{:S(2)}) %all-to-all-start) | async-done | bytes 32800 | tf_op jit(solution)/shard_map/all_to_all | solution.py:35
  22.1 0.2 multiply_reduce_fusion
  22.3 0.7 multiply_convert_fusion
  23.0 3.3 %all-to-all-start.1 = ((bf16[2,4,2048]{2,0,1:T(2,128)(2,1)}), bf16[2,4,2048]{2,0,1:T(2,128)(2,1)S(1)}, u32[]{:S(2)}, u32[]{:S(2)}) async-start(bf16[2,4,2048]{2,0,1:T(2,128)(2,1)} %multiply_convert_fusion), calls=%async_computation.1 | async-start | bytes 65536 | tf_op jit(solution)/shard_map/all_to_all | solution.py:121
  26.3 0.1 multiply_cosine_fusion
  27.1 4.8 %copy.46 = bf16[1,1024,2048]{2,1,0:T(8,128)(2,1)} copy(bf16[1,1024,2048]{2,1,0:T(8,128)(2,1)} %param.17) | data formatting | bytes 8388608
  31.9 0.0 all-to-all-done.1
  31.9 0.0 copy-start.6
  31.9 142.2 %collective-permute-done.2 = bf16[1,2048,256]{2,1,0:T(8,128)(2,1)} collective-permute-done((bf16[1,2048,256]{2,1,0:T(8,128)(2,1)S(1)}, bf16[1,2048,256]{2,1,0:T(8,128)(2,1)}, u32[]{:S(2)}, u32[]{:S(2)}) %collective-permute-start.2) | collective-permute-done | bytes 1048608 | tf_op jit(solution)/shard_map/ppermute | solution.py:22
  174.1 1.3 broadcast_select_fusion.4
  175.5 0.0 copy-start.3
  175.5 0.2 fusion.19
  175.7 20.0 %collective-permute-done.1 = bf16[1,2048,256]{2,1,0:T(8,128)(2,1)} collective-permute-done((bf16[1,2048,256]{2,1,0:T(8,128)(2,1)}, bf16[1,2048,256]{2,1,0:T(8,128)(2,1)}, u32[]{:S(2)}, u32[]{:S(2)}) %collective-permute-start.1) | collective-permute-done | bytes 1048608 | tf_op jit(solution)/shard_map/ppermute | solution.py:22
  195.8 1.3 broadcast_select_fusion.5
  197.1 0.0 copy-start.4
  197.1 0.2 fusion.21
  197.4 0.0 collective-permute-done
  197.4 2.7 broadcast_select_fusion
  200.1 0.0 copy-start.1
  200.1 0.7 fusion
  200.8 1.4 copy-done.1
  202.1 0.6 reshape.147
  202.8 3.3 %all-to-all-start.2 = ((f32[4,2,1536]{2,1,0:T(2,128)}), f32[4,2,1536]{2,1,0:T(2,128)S(1)}, u32[]{:S(2)}, u32[]{:S(2)}) async-start(f32[4,2,1536]{2,1,0:T(2,128)} %reshape.147), calls=%async_computation.2 | async-start | bytes 98304 | tf_op jit(solution)/shard_map/all_to_all | solution.py:40
  206.1 0.0 collective-permute-done.3
  206.1 5.0 %fusion.23 = (bf16[1,1024,2048]{2,1,0:T(8,128)(2,1)}, bf16[1,384,2048]{2,1,0:T(8,128)(2,1)}) fusion(bf16[1,1024,2048]{2,1,0:T(8,128)(2,1)} %copy.46, bf16[1,384,2048]{2,1,0:T(8,128)(2,1)} %collective-permute-done.3, pred[]{:T(512)S(6)} %and.15), kind=kLoop, calls=%fused_computation.27 | loop fusion | flops 786432 | bytes 7864321 | tf_op jit(solution)/shard_map/dynamic_update_slice | solution.py:114
  211.1 0.0 collective-permute-start.4
  211.1 0.0 all-to-all-done.2
  211.1 0.0 copy-start.8
  211.2 0.1 multiply_subtract_fusion
  211.3 0.1 fusion.53
  211.4 0.1 subtract_convert_fusion
  211.4 0.2 fusion.40
  211.6 0.8 select_reduce_fusion
  212.4 0.2 fusion.26
  212.7 0.1 copy-done.10
  212.8 0.4 fusion.14
  213.3 0.6 broadcast_in_dim.29
  213.9 3.2 %all-to-all-start.3 = ((bf16[4,2,1024]{2,1,0:T(2,128)(2,1)}), bf16[4,2,1024]{2,1,0:T(2,128)(2,1)S(1)}, u32[]{:S(2)}, u32[]{:S(2)}) async-start(bf16[4,2,1024]{2,1,0:T(2,128)(2,1)} %broadcast_in_dim.29), calls=%async_computation.3 | async-start | bytes 32768 | tf_op jit(solution)/shard_map/all_to_all | solution.py:35
  217.1 31.0 %collective-permute-done.4 = bf16[1,384,2048]{2,1,0:T(8,128)(2,1)} collective-permute-done((bf16[1,384,2048]{2,1,0:T(8,128)(2,1)}, bf16[1,384,2048]{2,1,0:T(8,128)(2,1)}, u32[]{:S(2)}, u32[]{:S(2)}) %collective-permute-start.4) | collective-permute-done | bytes 1572896 | tf_op jit(solution)/shard_map/ppermute | solution.py:22
  248.1 3.7 %fusion.24 = bf16[1,1024,2048]{2,1,0:T(8,128)(2,1)} fusion(bf16[1,1024,2048]{2,1,0:T(8,128)(2,1)} %get-tuple-element.7, bf16[1,384,2048]{2,1,0:T(8,128)(2,1)} %collective-permute-done.4, pred[]{:T(512)S(6)} %and.15, bf16[1,1024,2048]{2,1,0:T(8,128)(2,1)} %param.17), kind=kLoop, calls=%fused_computation.28 | loop fusion | flops 786432 | bytes 4718593 | tf_op jit(solution)/shard_map/dynamic_update_slice | solution.py:114
  251.9 2.2 fusion.8
  254.2 0.0 collective-permute-done.5
  254.2 1.9 fusion.17
  256.0 2.2 fusion.2
  258.2 0.7 all_to_all.40
  258.9 3.9 %all-to-all-start.4 = ((f32[4,2,2048]{2,1,0:T(2,128)}), f32[4,2,2048]{2,1,0:T(2,128)}, u32[]{:S(2)}, u32[]{:S(2)}) async-start(f32[4,2,2048]{2,1,0:T(2,128)} %all_to_all.40), calls=%async_computation.4 | async-start | bytes 131072 | tf_op jit(solution)/shard_map/all_to_all | solution.py:153
  262.8 2.9 %fusion.25 = bf16[1,1024,2048]{2,1,0:T(8,128)(2,1)} fusion(bf16[1,1024,2048]{2,1,0:T(8,128)(2,1)} %fusion.24, bf16[1,256,2048]{2,1,0:T(8,128)(2,1)} %collective-permute-done.5, pred[]{:T(512)S(6)} %and.15, bf16[1,1024,2048]{2,1,0:T(8,128)(2,1)} %param.17), kind=kLoop, calls=%fused_computation.29 | loop fusion | flops 524288 | bytes 3145729 | tf_op jit(solution)/shard_map/dynamic_update_slice | solution.py:114
  265.7 1.3 all-to-all-done.4
  267.0 5.1 %all-to-all-start.5 = ((f32[4,2,2048]{2,1,0:T(2,128)}), f32[4,2,2048]{2,1,0:T(2,128)S(1)}, u32[]{:S(2)}, u32[]{:S(2)}) async-start(f32[4,2,2048]{2,1,0:T(2,128)} %all-to-all-done.4), calls=%async_computation.5 | async-start | bytes 131072 | tf_op jit(solution)/shard_map/all_to_all | solution.py:40
  272.1 0.1 fusion.52
  272.1 0.6 copy.45
  272.7 5.1 %all-to-all-done.5 = f32[4,2,2048]{2,1,0:T(2,128)S(1)} async-done(((f32[4,2,2048]{2,1,0:T(2,128)}), f32[4,2,2048]{2,1,0:T(2,128)S(1)}, u32[]{:S(2)}, u32[]{:S(2)}) %all-to-all-start.5) | async-done | bytes 65568 | tf_op jit(solution)/shard_map/all_to_all | solution.py:40
  277.8 0.6 add_convert_fusion
  (34 shorter events, 0.3 us)
Async XLA Ops:
  0.6 211.0 %copy-start = (bf16[2,2048,256]{2,1,0:T(8,128)(2,1)S(1)}, bf16[2,2048,256]{2,1,0:T(8,128)(2,1)}, u32[]{:S(2)}) copy-start(bf16[2,2048,256]{2,1,0:T(8,128)(2,1)} %param.10) | copy-start | bytes 6291460
  0.6 10.3 %copy-start.7 = (bf16[2,2048]{1,0:T(2,128)(2,1)S(1)}, bf16[2,2048]{1,0:T(2,128)(2,1)}, u32[]{:S(2)}) copy-start(bf16[2,2048]{1,0:T(2,128)(2,1)} %param.9) | copy-start | bytes 24580
  0.7 15.8 %copy-start.5 = (bf16[1,2048,256]{2,1,0:T(8,128)(2,1)S(1)}, bf16[1,2048,256]{2,1,0:T(8,128)(2,1)}, u32[]{:S(2)}) copy-start(bf16[1,2048,256]{2,1,0:T(8,128)(2,1)} %param.16) | copy-start | bytes 3145732
  0.7 17.8 %copy-start.9 = (s32[2]{0:T(128)S(1)}, s32[2]{0:T(128)}, u32[]{:S(2)}) copy-start(s32[2]{0:T(128)} %param.12) | copy-start | bytes 28
  0.7 196.7 %collective-permute-start = (bf16[1,2048,1024]{2,1,0:T(8,128)(2,1)}, bf16[1,2048,1024]{2,1,0:T(8,128)(2,1)}, u32[]{:S(2)}, u32[]{:S(2)}) collective-permute-start(bf16[1,2048,1024]{2,1,0:T(8,128)(2,1)} %param.14), channel_id=1, source_target_pairs={{0,16},{16,0},{1,17},{17,1},{2,18},{18,2},{3,19},{19,3},{4,20},{20... | collective-permute-start | bytes 12582920 | tf_op jit(solution)/shard_map/ppermute | solution.py:22
  6.5 199.6 %collective-permute-start.3 = (bf16[1,384,2048]{2,1,0:T(8,128)(2,1)}, bf16[1,384,2048]{2,1,0:T(8,128)(2,1)}, u32[]{:S(2)}, u32[]{:S(2)}) collective-permute-start(bf16[1,384,2048]{2,1,0:T(8,128)(2,1)} %slice.80), channel_id=1, source_target_pairs={{0,16},{16,0},{1,17},{17,1},{2,18},{18,2},{3,19},{19,3},{4,20},{20... | collective-permute-start | bytes 4718600 | tf_op jit(solution)/shard_map/ppermute | solution.py:22
  9.1 245.1 %collective-permute-start.5 = (bf16[1,256,2048]{2,1,0:T(8,128)(2,1)}, bf16[1,256,2048]{2,1,0:T(8,128)(2,1)}, u32[]{:S(2)}, u32[]{:S(2)}) collective-permute-start(bf16[1,256,2048]{2,1,0:T(8,128)(2,1)} %slice.84), channel_id=1, source_target_pairs={{0,16},{16,0},{1,17},{17,1},{2,18},{18,2},{3,19},{19,3},{4,20},{20... | collective-permute-start | bytes 3145736 | tf_op jit(solution)/shard_map/ppermute | solution.py:22
  11.6 10.5 %all-to-all-start = ((bf16[4,2,2048]{2,1,0:T(2,128)(2,1)}), bf16[4,2,2048]{2,1,0:T(2,128)(2,1)S(1)}, u32[]{:S(2)}, u32[]{:S(2)}) async-start(bf16[4,2,2048]{2,1,0:T(2,128)(2,1)} %broadcast_in_dim.25), calls=%async_computation | async-start | bytes 65536 | tf_op jit(solution)/shard_map/all_to_all | solution.py:35
  16.4 157.7 %collective-permute-start.2 = (bf16[1,2048,256]{2,1,0:T(8,128)(2,1)S(1)}, bf16[1,2048,256]{2,1,0:T(8,128)(2,1)}, u32[]{:S(2)}, u32[]{:S(2)}) collective-permute-start(bf16[1,2048,256]{2,1,0:T(8,128)(2,1)S(1)} %copy-done.5), channel_id=1, source_target_pairs={{0,16},{16,0},{1,17},{17,1},{2,18},{18,2},{3,19},{19,3},{4,20},{20... | collective-permute-start | bytes 3145736 | tf_op jit(solution)/shard_map/ppermute | solution.py:22
  16.9 178.8 %collective-permute-start.1 = (bf16[1,2048,256]{2,1,0:T(8,128)(2,1)}, bf16[1,2048,256]{2,1,0:T(8,128)(2,1)}, u32[]{:S(2)}, u32[]{:S(2)}) collective-permute-start(bf16[1,2048,256]{2,1,0:T(8,128)(2,1)} %param.15), channel_id=1, source_target_pairs={{0,16},{16,0},{1,17},{17,1},{2,18},{18,2},{3,19},{19,3},{4,20},{20... | collective-permute-start | bytes 3145736 | tf_op jit(solution)/shard_map/ppermute | solution.py:22
  23.0 8.9 %all-to-all-start.1 = ((bf16[2,4,2048]{2,0,1:T(2,128)(2,1)}), bf16[2,4,2048]{2,0,1:T(2,128)(2,1)S(1)}, u32[]{:S(2)}, u32[]{:S(2)}) async-start(bf16[2,4,2048]{2,0,1:T(2,128)(2,1)} %multiply_convert_fusion), calls=%async_computation.1 | async-start | bytes 65536 | tf_op jit(solution)/shard_map/all_to_all | solution.py:121
  31.9 163.8 %copy-start.6 = (bf16[1,2048,256]{2,1,0:T(8,128)(2,1)S(1)}, bf16[1,2048,256]{2,1,0:T(8,128)(2,1)}, u32[]{:S(2)}) copy-start(bf16[1,2048,256]{2,1,0:T(8,128)(2,1)} %param.15) | copy-start | bytes 3145732
  175.5 21.6 %copy-start.3 = (bf16[1,2048,256]{2,1,0:T(8,128)(2,1)}, bf16[1,2048,256]{2,1,0:T(8,128)(2,1)S(1)}, u32[]{:S(2)}) copy-start(bf16[1,2048,256]{2,1,0:T(8,128)(2,1)S(1)} %broadcast_select_fusion.4) | copy-start | bytes 3145732
  175.7 21.6 %copy-start.2 = (bf16[1,2048,1024]{2,1,0:T(8,128)(2,1)S(1)}, bf16[1,2048,1024]{2,1,0:T(8,128)(2,1)}, u32[]{:S(2)}) copy-start(bf16[1,2048,1024]{2,1,0:T(8,128)(2,1)} %param.14) | copy-start | bytes 12582916
  197.1 3.0 %copy-start.4 = (bf16[1,2048,256]{2,1,0:T(8,128)(2,1)}, bf16[1,2048,256]{2,1,0:T(8,128)(2,1)S(1)}, u32[]{:S(2)}) copy-start(bf16[1,2048,256]{2,1,0:T(8,128)(2,1)S(1)} %broadcast_select_fusion.5) | copy-start | bytes 3145732
  200.1 2.0 copy-start.1
  202.8 8.3 %all-to-all-start.2 = ((f32[4,2,1536]{2,1,0:T(2,128)}), f32[4,2,1536]{2,1,0:T(2,128)S(1)}, u32[]{:S(2)}, u32[]{:S(2)}) async-start(f32[4,2,1536]{2,1,0:T(2,128)} %reshape.147), calls=%async_computation.2 | async-start | bytes 98304 | tf_op jit(solution)/shard_map/all_to_all | solution.py:40
  211.1 37.1 %collective-permute-start.4 = (bf16[1,384,2048]{2,1,0:T(8,128)(2,1)}, bf16[1,384,2048]{2,1,0:T(8,128)(2,1)}, u32[]{:S(2)}, u32[]{:S(2)}) collective-permute-start(bf16[1,384,2048]{2,1,0:T(8,128)(2,1)} %get-tuple-element.8), channel_id=1, source_target_pairs={{0,16},{16,0},{1,17},{17,1},{2,18},{18,2},{3,19},{19,3},{4,20},{20... | collective-permute-start | bytes 4718600 | tf_op jit(solution)/shard_map/ppermute | solution.py:22
  211.1 2.1 copy-start.8
  211.2 1.6 copy-start.10
  213.9 38.0 %all-to-all-start.3 = ((bf16[4,2,1024]{2,1,0:T(2,128)(2,1)}), bf16[4,2,1024]{2,1,0:T(2,128)(2,1)S(1)}, u32[]{:S(2)}, u32[]{:S(2)}) async-start(bf16[4,2,1024]{2,1,0:T(2,128)(2,1)} %broadcast_in_dim.29), calls=%async_computation.3 | async-start | bytes 32768 | tf_op jit(solution)/shard_map/all_to_all | solution.py:35
  258.9 8.1 %all-to-all-start.4 = ((f32[4,2,2048]{2,1,0:T(2,128)}), f32[4,2,2048]{2,1,0:T(2,128)}, u32[]{:S(2)}, u32[]{:S(2)}) async-start(f32[4,2,2048]{2,1,0:T(2,128)} %all_to_all.40), calls=%async_computation.4 | async-start | bytes 131072 | tf_op jit(solution)/shard_map/all_to_all | solution.py:153
  267.0 10.8 %all-to-all-start.5 = ((f32[4,2,2048]{2,1,0:T(2,128)}), f32[4,2,2048]{2,1,0:T(2,128)S(1)}, u32[]{:S(2)}, u32[]{:S(2)}) async-start(f32[4,2,2048]{2,1,0:T(2,128)} %all-to-all-done.4), calls=%async_computation.5 | async-start | bytes 131072 | tf_op jit(solution)/shard_map/all_to_all | solution.py:40
where the time goes:
time: 279 us; the launch traced here: 278 us
  waiting for transfers between devices  203 us (73%)
  starting transfers between devices  30.7 us (11%)
  other arithmetic  19.4 us (7%)
  local copies, waits for them, and re-layouts  14.7 us (5%)
  matrix products  8.86 us (3%)
    ppermute x6, waiting for transfers between devices, exchange(): received = lax.ppermute(shard, axis, pairs)  193 us
    dynamic_update_slice x3, other arithmetic, local(): fresh_out = lax.dynamic_update_slice(fresh_out, piece, (0, low, 0))  11.6 us
    all_to_all x2, starting transfers between devices, scatter_sum(): lax.all_to_all(terms, axis, split_axis=0, concat_axis=0, tiled=True)  8.36 us
    all_to_all x2, starting transfers between devices, gather(): lax.all_to_all(copies, axis, split_axis=0, concat_axis=0, tiled=True)  8.11 us
    ppermute x6, starting transfers between devices, exchange(): received = lax.ppermute(shard, axis, pairs)  7.11 us
    unnamed x26, local copies, waits for them, and re-layouts  6.89 us
    dot_general x3, matrix products, local(): jnp.dot(group_context[:, low:high], piece[0], preferred_element_type=jnp....  6.31 us
  transfers between devices with their start and end apart: 12, of which 6 were waited for; matrix products, arithmetic and copies ran while one was open for 13% of the time, Pallas kernels for 0%

commit v1 on v0

--- a/solution.py
+++ b/solution.py
@@ -1,6 +1,10 @@
+import functools
+
 import jax
 import jax.numpy as jnp
 from jax import lax
+from jax.experimental import pallas as pl
+from jax.experimental.pallas import tpu as pltpu
 from jax.sharding import PartitionSpec as P
 
 DH = 128
@@ -26,7 +30,7 @@
     return shard
 
 
-OUT_CUTS = (0, 3, 6, 8)
+OUT_CUTS = (0, 4, 7, 8)
 
 
 def gather(shard, axis, dim):
@@ -38,6 +42,112 @@
 
 def scatter_sum(terms, axis):
     return jnp.sum(lax.all_to_all(terms, axis, split_axis=0, concat_axis=0, tiled=True), axis=0)
+
+
+MESH = pl.DeviceIdType.MESH
+
+
+def deliver_kernel(ratio, part, out, land, send, recv, own_sem):
+    member = lax.axis_index("fs")
+    model = lax.axis_index("tp")
+    count = part.shape[0]
+    source = model // ratio
+    inner = source == member
+    barrier = pltpu.get_barrier_semaphore()
+    for i in range(count):
+
+        @pl.when(jnp.logical_not(inner & (model == i)))
+        def _():
+            pl.semaphore_signal(
+                barrier, inc=1, device_id={"tp": i, "fs": source}, device_id_type=MESH
+            )
+
+    @pl.when(inner)
+    def _():
+        pl.semaphore_wait(barrier, count - 1)
+
+    @pl.when(jnp.logical_not(inner))
+    def _():
+        pl.semaphore_wait(barrier, count)
+
+    def copy(k):
+        return pltpu.make_async_remote_copy(
+            src_ref=part.at[k],
+            dst_ref=land.at[model],
+            send_sem=send.at[k],
+            recv_sem=recv.at[model],
+            device_id={"tp": member * ratio + k % ratio, "fs": k // ratio},
+            device_id_type=MESH,
+        )
+
+    def here(k):
+        return (member == k // ratio) & (model == member * ratio + k % ratio)
+
+    def keep(k):
+        return pltpu.make_async_copy(part.at[k], land.at[model], own_sem)
+
+    for k in range(count):
+
+        @pl.when(jnp.logical_not(here(k)))
+        def _():
+            copy(k).start()
+
+        @pl.when(here(k))
+        def _():
+            keep(k).start()
+
+    for k in range(count):
+
+        @pl.when(jnp.logical_not(here(k)))
+        def _():
+            copy(k).wait_send()
+
+        @pl.when(here(k))
+        def _():
+            keep(k).wait()
+
+    for i in range(count):
+
+        @pl.when(jnp.logical_not(inner & (model == i)))
+        def _():
+            pltpu.make_async_remote_copy(
+                src_ref=part.at[0],
+                dst_ref=land.at[i],
+                send_sem=send.at[0],
+                recv_sem=recv.at[i],
+                device_id={"tp": i, "fs": source},
+                device_id_type=MESH,
+            ).wait_recv()
+
+    total = land[0]
+    for i in range(1, count):
+        total = total + land[i]
+    out[...] = total
+
+
+def deliver(partial_out, seqs):
+    members = lax.axis_size("fs")
+    models = lax.axis_size("tp")
+    if models % members:
+        terms = lax.all_to_all(partial_out, "fs", split_axis=0, concat_axis=1, tiled=True)
+        return scatter_sum(terms.reshape(seqs, models, -1).transpose(1, 0, 2), "tp")
+    ratio = models // members
+    width = partial_out.shape[1] // ratio
+    parts = partial_out.reshape(members, seqs, ratio, width).transpose(0, 2, 1, 3)
+    return pl.pallas_call(
+        functools.partial(deliver_kernel, ratio),
+        out_shape=jax.ShapeDtypeStruct((seqs, width), jnp.float32),
+        in_specs=[pl.BlockSpec(memory_space=pltpu.VMEM)],
+        out_specs=pl.BlockSpec(memory_space=pltpu.VMEM),
+        scratch_shapes=[
+            pltpu.VMEM((models, seqs, width), jnp.float32),
+            pltpu.SemaphoreType.DMA((models,)),
+            pltpu.SemaphoreType.DMA((models,)),
+            pltpu.SemaphoreType.DMA,
+        ],
+        compiler_params=pltpu.CompilerParams(collective_id=0, has_side_effects=True),
+        name="deliver",
+    )(parts.reshape(models, seqs, width))
 
 
 def rotate(heads, positions):
@@ -108,8 +218,9 @@
     fresh_query = exchange(query_weight, "rep", owner_rank)
     edges = [out_weight.shape[1] * cut // 8 for cut in OUT_CUTS]
     spans = list(zip(edges[:-1], edges[1:]))
-    out_pieces = [exchange(out_weight[:, low:high], "rep", owner_rank) for low, high in spans]
-    fresh_out = out_weight
+    held_pieces = lax.optimization_barrier([out_weight[:, low:high] for low, high in spans])
+    out_pieces = [exchange(piece, "rep", owner_rank) for piece in held_pieces]
+    normed, fresh_out = lax.optimization_barrier((normed, out_weight))
     for (low, high), piece in zip(spans, out_pieces):
         fresh_out = lax.dynamic_update_slice(fresh_out, piece, (0, low, 0))
     query_rows = fresh_query[0]
@@ -143,17 +254,18 @@
     context = attend(query_rot, key_new, value_new, cache_key, cache_value, lengths)
     context = context.astype(jnp.bfloat16).reshape(seqs, q_heads * DH)
     group_context = gather(context, "fs", 0)
-    partial_out = 0.0
+    partial_out = None
     for (low, high), piece in zip(spans, out_pieces):
-        partial_out = partial_out + jnp.dot(
+        term = jnp.dot(
             group_context[:, low:high],
             piece[0],
             preferred_element_type=jnp.float32,
         )
-    terms = lax.all_to_all(partial_out, "fs", split_axis=0, concat_axis=1, tiled=True)
-    model_groups = lax.axis_size("tp")
-    terms = terms.reshape(seqs, model_groups, -1).transpose(1, 0, 2)
-    summed = scatter_sum(terms, "tp")
+        if partial_out is None:
+            partial_out = term
+        else:
+            partial_out = lax.optimization_barrier(partial_out) + term
+    summed = deliver(partial_out, seqs)
     mixed = (summed + hidden.astype(jnp.float32)).astype(jnp.bfloat16)
     return (
         mixed,

time: 279 us -> 282 us (1.011)
  starting transfers between devices: 30.7 us -> 23.3 us
  Pallas kernels: 0 us -> 7.34 us
  waiting for transfers between devices: 203 us -> 210 us
  other arithmetic: 19.4 us -> 13.8 us
    pallas_call x0 -> x1, Pallas kernels: none -> 7.34 us  [deliver(): pl.pallas_call(functools.partial(deliver_kernel, ratio), out_shape=jax.Sh...]
    ppermute x6, waiting for transfers between devices: 193 us -> 200 us  [exchange(): received = lax.ppermute(shard, axis, pairs)]
    dynamic_update_slice x3, other arithmetic: 11.6 us -> 5.47 us  [local(): fresh_out = lax.dynamic_update_slice(fresh_out, piece, (0, low, 0))]
    all_to_all x2 -> x1, starting transfers between devices: 8.36 us -> 3.27 us  [scatter_sum(): lax.all_to_all(terms, axis, split_axis=0, concat_axis=0, tiled=True)]
    optimization_barrier x0 -> x1, local copies, waits for them, and re-layouts: none -> 4.94 us  [local(): normed, fresh_out = lax.optimization_barrier((normed, out_weight))]
    all_to_all x1 -> x0, starting transfers between devices: 3.89 us -> none  [local(): lax.all_to_all(partial_out, 'fs', split_axis=0, concat_axis=1, tiled=True)]
    all_to_all x1, waiting for transfers between devices: 0.01 us -> 3.12 us  [local(): lax.all_to_all(normed, 'fs', split_axis=1, concat_axis=0, tiled=True)]
    unnamed x26 -> x25, local copies, waits for them, and re-layouts: 6.89 us -> 4.7 us
  transfers between devices with their start and end apart: 12 -> 10, of which waited for: 6 -> 5; matrix products, arithmetic and copies ran while one was open for 13% -> 7% of each run, Pallas kernels for 0% -> 0%
where the time goes in v1:
time: 282 us; the launch traced here: 281 us
  waiting for transfers between devices  210 us (74%)
  starting transfers between devices  23.3 us (8%)
  local copies, waits for them, and re-layouts  17 us (6%)
  other arithmetic  13.8 us (5%)
  matrix products  8.18 us (3%)
  Pallas kernels  7.34 us (3%)
    ppermute x6, waiting for transfers between devices, exchange(): received = lax.ppermute(shard, axis, pairs)  200 us
    all_to_all x2, starting transfers between devices, gather(): lax.all_to_all(copies, axis, split_axis=0, concat_axis=0, tiled=True)  9.58 us
    pallas_call x1, Pallas kernels, deliver(): pl.pallas_call(functools.partial(deliver_kernel, ratio), out_shape=jax.Sh...  7.34 us
    ppermute x6, starting transfers between devices, exchange(): received = lax.ppermute(shard, axis, pairs)  7.16 us
  transfers between devices with their start and end apart: 10, of which 5 were waited for; matrix products, arithmetic and copies ran while one was open for 7% of the time, Pallas kernels for 0%

profile of v1, /device:TPU:0, one launch (start us, length us, event | category | flops | bytes accessed | tf_op | source)
XLA Modules:
  0.0 281.0 jit_solution(17334554498804659941)
XLA Ops:
  0.6 0.0 copy-start
  0.7 4.9 %copy.53 = bf16[1,1024,2048]{2,1,0:T(8,128)(2,1)} copy(bf16[1,1024,2048]{2,1,0:T(8,128)(2,1)} %param.17) | data formatting | bytes 8388608 | tf_op jit(solution)/shard_map/optimization_barrier | solution.py:223
  5.6 0.6 broadcast_in_dim.25
  6.2 6.3 %all-to-all-start = ((bf16[4,2,2048]{2,1,0:T(2,128)(2,1)}), bf16[4,2,2048]{2,1,0:T(2,128)(2,1)S(1)}, u32[]{:S(2)}, u32[]{:S(2)}) async-start(bf16[4,2,2048]{2,1,0:T(2,128)(2,1)} %broadcast_in_dim.25), calls=%async_computation | async-start | bytes 65536 | tf_op jit(solution)/shard_map/all_to_all | solution.py:39
  12.6 3.3 %slice.80 = bf16[1,512,2048]{2,1,0:T(8,128)(2,1)} slice(bf16[1,1024,2048]{2,1,0:T(8,128)(2,1)} %copy.53), slice={[0:1], [0:512], [0:2048]} | slice | bytes 4194304 | tf_op jit(solution)/shard_map/slice | solution.py:221
  15.9 1.3 slice.81
  17.3 1.6 collective-permute-start.3
  18.9 0.5 collective-permute-start.4
  19.4 1.5 collective-permute-start
  20.9 0.5 collective-permute-start.2
  21.4 1.5 collective-permute-start.1
  22.9 0.1 iota_compare_fusion
  23.0 0.0 all-to-all-done
  23.1 0.2 fusion.27
  23.3 0.7 fusion.28
  24.0 3.3 %all-to-all-start.1 = ((bf16[2,4,2048]{2,0,1:T(2,128)(2,1)}), bf16[2,4,2048]{2,0,1:T(2,128)(2,1)S(1)}, u32[]{:S(2)}, u32[]{:S(2)}) async-start(bf16[2,4,2048]{2,0,1:T(2,128)(2,1)} %bitcast.4), calls=%async_computation.1 | async-start | bytes 65536 | tf_op jit(solution)/shard_map/all_to_all | solution.py:232
  27.3 0.1 multiply_cosine_fusion
  28.1 3.1 %all-to-all-done.1 = bf16[2,4,2048]{2,0,1:T(2,128)(2,1)S(1)} async-done(((bf16[2,4,2048]{2,0,1:T(2,128)(2,1)}), bf16[2,4,2048]{2,0,1:T(2,128)(2,1)S(1)}, u32[]{:S(2)}, u32[]{:S(2)}) %all-to-all-start.1) | async-done | bytes 32800 | tf_op jit(solution)/shard_map/all_to_all | solution.py:232
  31.2 181.0 %collective-permute-done.2 = bf16[1,2048,256]{2,1,0:T(8,128)(2,1)} collective-permute-done((bf16[1,2048,256]{2,1,0:T(8,128)(2,1)}, bf16[1,2048,256]{2,1,0:T(8,128)(2,1)}, u32[]{:S(2)}, u32[]{:S(2)}) %collective-permute-start.2) | collective-permute-done | bytes 1048608 | tf_op jit(solution)/shard_map/ppermute | solution.py:26
  212.2 1.5 collective-permute-start.5
  213.7 1.3 broadcast_select_fusion.3
  215.1 0.0 copy-start.6
  215.1 0.2 fusion.17
  215.3 19.4 %collective-permute-done.1 = bf16[1,2048,256]{2,1,0:T(8,128)(2,1)} collective-permute-done((bf16[1,2048,256]{2,1,0:T(8,128)(2,1)}, bf16[1,2048,256]{2,1,0:T(8,128)(2,1)}, u32[]{:S(2)}, u32[]{:S(2)}) %collective-permute-start.1) | collective-permute-done | bytes 1048608 | tf_op jit(solution)/shard_map/ppermute | solution.py:26
  234.7 1.3 broadcast_select_fusion.4
  236.0 0.0 copy-start.7
  236.1 0.2 fusion.19
  236.3 0.7 copy-done.7
  237.0 0.0 collective-permute-done.3
  237.0 2.4 fusion.21
  239.4 0.0 copy-start.5
  239.4 0.0 collective-permute-done.4
  239.4 2.2 fusion.22
  241.6 0.0 copy-start.4
  241.6 2.0 copy-done.4
  243.6 0.0 collective-permute-done
  243.6 2.6 broadcast_select_fusion
  246.3 0.0 copy-start.1
  246.3 0.7 fusion
  246.9 1.4 copy-done.1
  248.3 0.6 reshape.129
  248.9 3.3 %all-to-all-start.2 = ((f32[4,2,1536]{2,1,0:T(2,128)}), f32[4,2,1536]{2,1,0:T(2,128)S(1)}, u32[]{:S(2)}, u32[]{:S(2)}) async-start(f32[4,2,1536]{2,1,0:T(2,128)} %reshape.129), calls=%async_computation.2 | async-start | bytes 98304 | tf_op jit(solution)/shard_map/all_to_all | solution.py:44
  252.2 0.0 collective-permute-done.5
  252.2 0.9 fusion.25
  253.1 3.1 %all-to-all-done.2 = f32[4,2,1536]{2,1,0:T(2,128)S(1)} async-done(((f32[4,2,1536]{2,1,0:T(2,128)}), f32[4,2,1536]{2,1,0:T(2,128)S(1)}, u32[]{:S(2)}, u32[]{:S(2)}) %all-to-all-start.2) | async-done | bytes 49184 | tf_op jit(solution)/shard_map/all_to_all | solution.py:44
  256.3 0.0 copy-start.9
  256.3 0.1 multiply_subtract_fusion
  256.4 0.1 subtract_convert_fusion
  256.5 0.1 fusion.52
  256.5 0.2 fusion.42
  256.7 0.8 select_reduce_fusion
  257.5 0.2 fusion.26
  257.8 2.0 fusion.14
  259.8 0.6 broadcast_in_dim.29
  260.5 3.2 %all-to-all-start.3 = ((bf16[4,2,1024]{2,1,0:T(2,128)(2,1)}), bf16[4,2,1024]{2,1,0:T(2,128)(2,1)S(1)}, u32[]{:S(2)}, u32[]{:S(2)}) async-start(bf16[4,2,1024]{2,1,0:T(2,128)(2,1)} %broadcast_in_dim.29), calls=%async_computation.3 | async-start | bytes 32768 | tf_op jit(solution)/shard_map/all_to_all | solution.py:39
  263.7 0.1 fusion.51
  263.8 0.6 copy.47
  264.3 3.2 %all-to-all-done.3 = bf16[4,2,1024]{2,1,0:T(2,128)(2,1)S(1)} async-done(((bf16[4,2,1024]{2,1,0:T(2,128)(2,1)}), bf16[4,2,1024]{2,1,0:T(2,128)(2,1)S(1)}, u32[]{:S(2)}, u32[]{:S(2)}) %all-to-all-start.3) | async-done | bytes 16416 | tf_op jit(solution)/shard_map/all_to_all | solution.py:39
  267.6 2.1 fusion.7
  269.6 1.8 fusion.9
  271.4 0.2 fusion.23
  271.6 0.7 reshape_transpose_reshape.3.part
  272.3 7.3 %deliver.1 = f32[2,2048]{1,0:T(2,128)} custom-call(f32[4,2,2048]{2,1,0:T(2,128)} %reshape_transpose_reshape.3.part), custom_call_target="tpu_custom_call" | custom-call | tf_op jit(solution)/shard_map/deliver/pallas_call | solution.py:137
  279.7 1.3 add_convert_fusion
  (33 shorter events, 0.3 us)
Async XLA Ops:
  0.6 256.1 %copy-start = (bf16[2,2048,256]{2,1,0:T(8,128)(2,1)S(1)}, bf16[2,2048,256]{2,1,0:T(8,128)(2,1)}, u32[]{:S(2)}) copy-start(bf16[2,2048,256]{2,1,0:T(8,128)(2,1)} %param.10) | copy-start | bytes 6291460
  0.6 5.0 %copy-start.8 = (bf16[2,2048]{1,0:T(2,128)(2,1)S(1)}, bf16[2,2048]{1,0:T(2,128)(2,1)}, u32[]{:S(2)}) copy-start(bf16[2,2048]{1,0:T(2,128)(2,1)} %param.9) | copy-start | bytes 24580
  6.2 16.8 %all-to-all-start = ((bf16[4,2,2048]{2,1,0:T(2,128)(2,1)}), bf16[4,2,2048]{2,1,0:T(2,128)(2,1)S(1)}, u32[]{:S(2)}, u32[]{:S(2)}) async-start(bf16[4,2,2048]{2,1,0:T(2,128)(2,1)} %broadcast_in_dim.25), calls=%async_computation | async-start | bytes 65536 | tf_op jit(solution)/shard_map/all_to_all | solution.py:39
  12.6 3.3 %copy-start.2 = (bf16[1,1024,2048]{2,1,0:T(8,128)(2,1)S(1)}, bf16[1,1024,2048]{2,1,0:T(8,128)(2,1)}, u32[]{:S(2)}) copy-start(bf16[1,1024,2048]{2,1,0:T(8,128)(2,1)} %copy.53) | copy-start | bytes 12582916
  15.9 7.0 %copy-start.10 = (s32[2]{0:T(128)S(1)}, s32[2]{0:T(128)}, u32[]{:S(2)}) copy-start(s32[2]{0:T(128)} %param.12) | copy-start | bytes 28
  17.3 219.7 %collective-permute-start.3 = (bf16[1,512,2048]{2,1,0:T(8,128)(2,1)}, bf16[1,512,2048]{2,1,0:T(8,128)(2,1)}, u32[]{:S(2)}, u32[]{:S(2)}) collective-permute-start(bf16[1,512,2048]{2,1,0:T(8,128)(2,1)} %slice.80), channel_id=1, source_target_pairs={{0,16},{16,0},{1,17},{17,1},{2,18},{18,2},{3,19},{19,3},{4,20},{20... | collective-permute-start | bytes 6291464 | tf_op jit(solution)/shard_map/ppermute | solution.py:26
  18.9 220.6 %collective-permute-start.4 = (bf16[1,384,2048]{2,1,0:T(8,128)(2,1)}, bf16[1,384,2048]{2,1,0:T(8,128)(2,1)}, u32[]{:S(2)}, u32[]{:S(2)}) collective-permute-start(bf16[1,384,2048]{2,1,0:T(8,128)(2,1)} %slice.81), channel_id=1, source_target_pairs={{0,16},{16,0},{1,17},{17,1},{2,18},{18,2},{3,19},{19,3},{4,20},{20... | collective-permute-start | bytes 4718600 | tf_op jit(solution)/shard_map/ppermute | solution.py:26
  19.4 224.3 %collective-permute-start = (bf16[1,2048,1024]{2,1,0:T(8,128)(2,1)}, bf16[1,2048,1024]{2,1,0:T(8,128)(2,1)}, u32[]{:S(2)}, u32[]{:S(2)}) collective-permute-start(bf16[1,2048,1024]{2,1,0:T(8,128)(2,1)} %param.14), channel_id=1, source_target_pairs={{0,16},{16,0},{1,17},{17,1},{2,18},{18,2},{3,19},{19,3},{4,20},{20... | collective-permute-start | bytes 12582920 | tf_op jit(solution)/shard_map/ppermute | solution.py:26
  20.9 191.3 %collective-permute-start.2 = (bf16[1,2048,256]{2,1,0:T(8,128)(2,1)}, bf16[1,2048,256]{2,1,0:T(8,128)(2,1)}, u32[]{:S(2)}, u32[]{:S(2)}) collective-permute-start(bf16[1,2048,256]{2,1,0:T(8,128)(2,1)} %param.16), channel_id=1, source_target_pairs={{0,16},{16,0},{1,17},{17,1},{2,18},{18,2},{3,19},{19,3},{4,20},{20... | collective-permute-start | bytes 3145736 | tf_op jit(solution)/shard_map/ppermute | solution.py:26
  21.4 213.3 %collective-permute-start.1 = (bf16[1,2048,256]{2,1,0:T(8,128)(2,1)}, bf16[1,2048,256]{2,1,0:T(8,128)(2,1)}, u32[]{:S(2)}, u32[]{:S(2)}) collective-permute-start(bf16[1,2048,256]{2,1,0:T(8,128)(2,1)} %param.15), channel_id=1, source_target_pairs={{0,16},{16,0},{1,17},{17,1},{2,18},{18,2},{3,19},{19,3},{4,20},{20... | collective-permute-start | bytes 3145736 | tf_op jit(solution)/shard_map/ppermute | solution.py:26
  24.0 7.2 %all-to-all-start.1 = ((bf16[2,4,2048]{2,0,1:T(2,128)(2,1)}), bf16[2,4,2048]{2,0,1:T(2,128)(2,1)S(1)}, u32[]{:S(2)}, u32[]{:S(2)}) async-start(bf16[2,4,2048]{2,0,1:T(2,128)(2,1)} %bitcast.4), calls=%async_computation.1 | async-start | bytes 65536 | tf_op jit(solution)/shard_map/all_to_all | solution.py:232
  212.2 40.0 %collective-permute-start.5 = (bf16[1,128,2048]{2,1,0:T(8,128)(2,1)S(1)}, bf16[1,128,2048]{2,1,0:T(8,128)(2,1)S(1)}, u32[]{:S(2)}, u32[]{:S(2)}) collective-permute-start(bf16[1,128,2048]{2,1,0:T(8,128)(2,1)S(1)} %slice.82), channel_id=1, source_target_pairs={{0,16},{16,0},{1,17},{17,1},{2,18},{18,2},{3,19},{19,3},{4,20},{20... | collective-permute-start | bytes 1572872 | tf_op jit(solution)/shard_map/ppermute | solution.py:26
  215.1 21.0 %copy-start.6 = (bf16[1,2048,256]{2,1,0:T(8,128)(2,1)}, bf16[1,2048,256]{2,1,0:T(8,128)(2,1)S(1)}, u32[]{:S(2)}) copy-start(bf16[1,2048,256]{2,1,0:T(8,128)(2,1)S(1)} %broadcast_select_fusion.3) | copy-start | bytes 3145732
  215.3 21.7 %copy-start.3 = (bf16[1,1024,2048]{2,1,0:T(8,128)(2,1)S(1)}, bf16[1,1024,2048]{2,1,0:T(8,128)(2,1)}, u32[]{:S(2)}) copy-start(bf16[1,1024,2048]{2,1,0:T(8,128)(2,1)} %copy.53) | copy-start | bytes 12582916
  236.0 1.0 copy-start.7
  239.4 4.2 %copy-start.5 = (bf16[1,2048,1024]{2,1,0:T(8,128)(2,1)S(1)}, bf16[1,2048,1024]{2,1,0:T(8,128)(2,1)}, u32[]{:S(2)}) copy-start(bf16[1,2048,1024]{2,1,0:T(8,128)(2,1)} %param.14) | copy-start | bytes 12582916
  241.6 2.0 copy-start.4
  246.3 2.0 copy-start.1
  248.9 7.3 %all-to-all-start.2 = ((f32[4,2,1536]{2,1,0:T(2,128)}), f32[4,2,1536]{2,1,0:T(2,128)S(1)}, u32[]{:S(2)}, u32[]{:S(2)}) async-start(f32[4,2,1536]{2,1,0:T(2,128)} %reshape.129), calls=%async_computation.2 | async-start | bytes 98304 | tf_op jit(solution)/shard_map/all_to_all | solution.py:44
  256.3 3.5 %copy-start.9 = (bf16[2,256]{1,0:T(2,128)(2,1)}, bf16[2,256]{1,0:T(2,128)(2,1)S(1)}, u32[]{:S(2)}) copy-start(bf16[2,256]{1,0:T(2,128)(2,1)S(1)} %slice.124) | copy-start | bytes 3076
  260.5 7.1 %all-to-all-start.3 = ((bf16[4,2,1024]{2,1,0:T(2,128)(2,1)}), bf16[4,2,1024]{2,1,0:T(2,128)(2,1)S(1)}, u32[]{:S(2)}, u32[]{:S(2)}) async-start(bf16[4,2,1024]{2,1,0:T(2,128)(2,1)} %broadcast_in_dim.29), calls=%async_computation.3 | async-start | bytes 32768 | tf_op jit(solution)/shard_map/all_to_all | solution.py:39

commit v2 on v1

--- a/solution.py
+++ b/solution.py
@@ -220,8 +220,11 @@
     spans = list(zip(edges[:-1], edges[1:]))
     held_pieces = lax.optimization_barrier([out_weight[:, low:high] for low, high in spans])
     out_pieces = [exchange(piece, "rep", owner_rank) for piece in held_pieces]
-    normed, fresh_out = lax.optimization_barrier((normed, out_weight))
-    for (low, high), piece in zip(spans, out_pieces):
+    first_rows = edges[1]
+    rows = lax.broadcasted_iota(jnp.int32, out_weight.shape, 1)
+    padded = jnp.pad(out_pieces[0], ((0, 0), (0, out_weight.shape[1] - first_rows), (0, 0)))
+    fresh_out = jnp.where(rows < first_rows, padded, out_weight)
+    for (low, high), piece in zip(spans[1:], out_pieces[1:]):
         fresh_out = lax.dynamic_update_slice(fresh_out, piece, (0, low, 0))
     query_rows = fresh_query[0]
     key_rows = fresh_key[0]

time: 282 us -> 275 us (0.975)
  waiting for transfers between devices: 210 us -> 204 us
  local copies, waits for them, and re-layouts: 17 us -> 12.6 us
  other arithmetic: 13.8 us -> 17.1 us
    ppermute x6, waiting for transfers between devices: 200 us -> 191 us  [exchange(): received = lax.ppermute(shard, axis, pairs)]
    optimization_barrier x1 -> x0, local copies, waits for them, and re-layouts: 4.94 us -> none  [local(): normed, fresh_out = lax.optimization_barrier((normed, out_weight))]
    select_n x0 -> x1, other arithmetic: none -> 3.61 us  [local(): fresh_out = jnp.where(rows < first_rows, padded, out_weight)]
    all_to_all x2, waiting for transfers between devices: 3.18 us -> 6.59 us  [gather(): lax.all_to_all(copies, axis, split_axis=0, concat_axis=0, tiled=True)]
    select_n x3 -> x4, other arithmetic: 5.3 us -> 7.26 us  [exchange(): shard = jnp.where(takes, received, shard)]
  transfers between devices with their start and end apart: 10 -> 10, of which waited for: 5 -> 6; matrix products, arithmetic and copies ran while one was open for 7% -> 7% of each run, Pallas kernels for 0% -> 0%
where the time goes in v2:
time: 275 us; the launch traced here: 274 us
  waiting for transfers between devices  204 us (74%)
  starting transfers between devices  23.8 us (9%)
  other arithmetic  17.1 us (6%)
  local copies, waits for them, and re-layouts  12.6 us (5%)
  matrix products  8.08 us (3%)
  Pallas kernels  7.6 us (3%)
    ppermute x6, waiting for transfers between devices, exchange(): received = lax.ppermute(shard, axis, pairs)  191 us
    ppermute x6, starting transfers between devices, exchange(): received = lax.ppermute(shard, axis, pairs)  9.13 us
    all_to_all x2, starting transfers between devices, gather(): lax.all_to_all(copies, axis, split_axis=0, concat_axis=0, tiled=True)  8.11 us
    pallas_call x1, Pallas kernels, deliver(): pl.pallas_call(functools.partial(deliver_kernel, ratio), out_shape=jax.Sh...  7.6 us
    select_n x4, other arithmetic, exchange(): shard = jnp.where(takes, received, shard)  7.26 us
    all_to_all x2, waiting for transfers between devices, gather(): lax.all_to_all(copies, axis, split_axis=0, concat_axis=0, tiled=True)  6.59 us
  transfers between devices with their start and end apart: 10, of which 6 were waited for; matrix products, arithmetic and copies ran while one was open for 7% of the time, Pallas kernels for 0%

profile of v2, /device:TPU:0, one launch (start us, length us, event | category | flops | bytes accessed | tf_op | source)
XLA Modules:
  0.0 274.2 jit_solution(15131601669294505775)
XLA Ops:
  0.6 0.0 copy-start
  0.6 0.0 copy-start.2
  0.7 3.3 %slice.80 = bf16[1,512,2048]{2,1,0:T(8,128)(2,1)} slice(bf16[1,1024,2048]{2,1,0:T(8,128)(2,1)} %param.17), slice={[0:1], [0:512], [0:2048]} | slice | bytes 4194304 | tf_op jit(solution)/shard_map/slice | solution.py:221
  4.0 1.3 slice.81
  5.3 3.1 %collective-permute-start.3 = (bf16[1,512,2048]{2,1,0:T(8,128)(2,1)}, bf16[1,512,2048]{2,1,0:T(8,128)(2,1)}, u32[]{:S(2)}, u32[]{:S(2)}) collective-permute-start(bf16[1,512,2048]{2,1,0:T(8,128)(2,1)} %slice.80), channel_id=1, source_target_pairs={{0,16},{16,0},{1,17},{17,1},{2,18},{18,2},{3,19},{19,3},{4,20},{20... | collective-permute-start | bytes 6291464 | tf_op jit(solution)/shard_map/ppermute | solution.py:26
  8.3 0.1 collective-permute-start.4
  8.4 1.9 collective-permute-start
  10.4 0.6 broadcast_in_dim.25
  11.0 4.9 %all-to-all-start = ((bf16[4,2,2048]{2,1,0:T(2,128)(2,1)}), bf16[4,2,2048]{2,1,0:T(2,128)(2,1)S(1)}, u32[]{:S(2)}, u32[]{:S(2)}) async-start(bf16[4,2,2048]{2,1,0:T(2,128)(2,1)} %broadcast_in_dim.25), calls=%async_computation | async-start | bytes 65536 | tf_op jit(solution)/shard_map/all_to_all | solution.py:39
  15.9 0.5 collective-permute-start.2
  16.4 1.5 collective-permute-start.1
  17.9 0.1 iota_compare_fusion
  18.0 0.1 multiply_cosine_fusion
  18.1 3.4 %all-to-all-done = bf16[4,2,2048]{2,1,0:T(2,128)(2,1)S(1)} async-done(((bf16[4,2,2048]{2,1,0:T(2,128)(2,1)}), bf16[4,2,2048]{2,1,0:T(2,128)(2,1)S(1)}, u32[]{:S(2)}, u32[]{:S(2)}) %all-to-all-start) | async-done | bytes 32800 | tf_op jit(solution)/shard_map/all_to_all | solution.py:39
  21.6 0.2 multiply_reduce_fusion
  21.8 0.7 multiply_convert_fusion
  22.5 3.3 %all-to-all-start.1 = ((bf16[2,4,2048]{2,0,1:T(2,128)(2,1)}), bf16[2,4,2048]{2,0,1:T(2,128)(2,1)S(1)}, u32[]{:S(2)}, u32[]{:S(2)}) async-start(bf16[2,4,2048]{2,0,1:T(2,128)(2,1)} %multiply_convert_fusion), calls=%async_computation.1 | async-start | bytes 65536 | tf_op jit(solution)/shard_map/all_to_all | solution.py:235
  26.4 3.2 %all-to-all-done.1 = bf16[2,4,2048]{2,0,1:T(2,128)(2,1)S(1)} async-done(((bf16[2,4,2048]{2,0,1:T(2,128)(2,1)}), bf16[2,4,2048]{2,0,1:T(2,128)(2,1)S(1)}, u32[]{:S(2)}, u32[]{:S(2)}) %all-to-all-start.1) | async-done | bytes 32800 | tf_op jit(solution)/shard_map/all_to_all | solution.py:235
  29.7 0.0 copy-start.9
  29.7 171.5 %collective-permute-done.2 = bf16[1,2048,256]{2,1,0:T(8,128)(2,1)} collective-permute-done((bf16[1,2048,256]{2,1,0:T(8,128)(2,1)}, bf16[1,2048,256]{2,1,0:T(8,128)(2,1)}, u32[]{:S(2)}, u32[]{:S(2)}) %collective-permute-start.2) | collective-permute-done | bytes 1048608 | tf_op jit(solution)/shard_map/ppermute | solution.py:26
  201.2 2.0 collective-permute-start.5
  203.2 1.3 broadcast_select_fusion.3
  204.6 0.0 copy-start.7
  204.6 19.1 %collective-permute-done.1 = bf16[1,2048,256]{2,1,0:T(8,128)(2,1)} collective-permute-done((bf16[1,2048,256]{2,1,0:T(8,128)(2,1)}, bf16[1,2048,256]{2,1,0:T(8,128)(2,1)}, u32[]{:S(2)}, u32[]{:S(2)}) %collective-permute-start.1) | collective-permute-done | bytes 1048608 | tf_op jit(solution)/shard_map/ppermute | solution.py:26
  223.7 1.3 broadcast_select_fusion.4
  225.0 0.0 copy-start.8
  225.0 0.2 fusion.17
  225.3 0.3 fusion.19
  225.5 0.5 copy-done.8
  226.0 2.0 broadcast_select_fusion.1
  228.0 0.8 copy-done.3
  228.8 3.6 %pad_select_fusion = bf16[1,1024,2048]{2,1,0:T(8,128)(2,1)S(1)} fusion(bf16[1,1024,2048]{2,1,0:T(8,128)(2,1)S(1)} %copy-done.3, bf16[1,512,2048]{2,1,0:T(8,128)(2,1)S(1)} %broadcast_select_fusion.1, pred[1024]{0:T(1024)(128)(4,1)S(1)} %iota_compare_fusion.1), kind=kLoop, calls=%fused_computation.2 | loop fusion | flops 2097152 | bytes 10486784 | tf_op jit(solution)/shard_map/jit(_where)/select_n | solution.py:226
  232.4 0.0 copy-start.5
  232.5 2.2 fusion.21
  234.7 0.0 copy-start.6
  234.7 2.0 copy-done.6
  236.7 0.0 collective-permute-done
  236.7 2.6 broadcast_select_fusion
  239.4 0.0 copy-start.4
  239.4 0.7 fusion
  240.0 1.4 copy-done.4
  241.4 0.6 reshape.142
  242.0 3.3 %all-to-all-start.2 = ((f32[4,2,1536]{2,1,0:T(2,128)}), f32[4,2,1536]{2,1,0:T(2,128)S(1)}, u32[]{:S(2)}, u32[]{:S(2)}) async-start(f32[4,2,1536]{2,1,0:T(2,128)} %reshape.142), calls=%async_computation.2 | async-start | bytes 98304 | tf_op jit(solution)/shard_map/all_to_all | solution.py:44
  245.3 0.9 fusion.24
  246.2 3.1 %all-to-all-done.2 = f32[4,2,1536]{2,1,0:T(2,128)S(1)} async-done(((f32[4,2,1536]{2,1,0:T(2,128)}), f32[4,2,1536]{2,1,0:T(2,128)S(1)}, u32[]{:S(2)}, u32[]{:S(2)}) %all-to-all-start.2) | async-done | bytes 49184 | tf_op jit(solution)/shard_map/all_to_all | solution.py:44
  249.4 0.0 copy-start.11
  249.4 0.1 multiply_subtract_fusion
  249.5 0.1 subtract_convert_fusion
  249.6 0.1 fusion.49
  249.6 0.2 fusion.39
  249.8 0.8 select_reduce_fusion
  250.6 0.2 fusion.25
  250.9 2.0 fusion.14
  252.9 0.6 broadcast_in_dim.29
  253.5 3.2 %all-to-all-start.3 = ((bf16[4,2,1024]{2,1,0:T(2,128)(2,1)}), bf16[4,2,1024]{2,1,0:T(2,128)(2,1)S(1)}, u32[]{:S(2)}, u32[]{:S(2)}) async-start(bf16[4,2,1024]{2,1,0:T(2,128)(2,1)} %broadcast_in_dim.29), calls=%async_computation.3 | async-start | bytes 32768 | tf_op jit(solution)/shard_map/all_to_all | solution.py:39
  256.8 0.1 fusion.48
  256.9 0.6 copy.45
  257.4 3.2 %all-to-all-done.3 = bf16[4,2,1024]{2,1,0:T(2,128)(2,1)S(1)} async-done(((bf16[4,2,1024]{2,1,0:T(2,128)(2,1)}), bf16[4,2,1024]{2,1,0:T(2,128)(2,1)S(1)}, u32[]{:S(2)}, u32[]{:S(2)}) %all-to-all-start.3) | async-done | bytes 16416 | tf_op jit(solution)/shard_map/all_to_all | solution.py:39
  260.7 2.0 fusion.7
  262.6 1.8 fusion.9
  264.4 0.2 fusion.22
  264.6 0.7 reshape_transpose_reshape.3.part
  265.3 7.6 %deliver.1 = f32[2,2048]{1,0:T(2,128)} custom-call(f32[4,2,2048]{2,1,0:T(2,128)} %reshape_transpose_reshape.3.part), custom_call_target="tpu_custom_call" | custom-call | tf_op jit(solution)/shard_map/deliver/pallas_call | solution.py:137
  272.9 1.3 add_convert_fusion
  (38 shorter events, 0.3 us)
Async XLA Ops:
  0.6 249.2 %copy-start = (bf16[2,2048,256]{2,1,0:T(8,128)(2,1)S(1)}, bf16[2,2048,256]{2,1,0:T(8,128)(2,1)}, u32[]{:S(2)}) copy-start(bf16[2,2048,256]{2,1,0:T(8,128)(2,1)} %param.10) | copy-start | bytes 6291460
  0.6 3.3 %copy-start.2 = (bf16[1,1024,2048]{2,1,0:T(8,128)(2,1)S(1)}, bf16[1,1024,2048]{2,1,0:T(8,128)(2,1)}, u32[]{:S(2)}) copy-start(bf16[1,1024,2048]{2,1,0:T(8,128)(2,1)} %param.17) | copy-start | bytes 12582916
  4.0 6.4 %copy-start.10 = (bf16[2,2048]{1,0:T(2,128)(2,1)S(1)}, bf16[2,2048]{1,0:T(2,128)(2,1)}, u32[]{:S(2)}) copy-start(bf16[2,2048]{1,0:T(2,128)(2,1)} %param.9) | copy-start | bytes 24580
  4.0 13.9 %copy-start.12 = (s32[2]{0:T(128)S(1)}, s32[2]{0:T(128)}, u32[]{:S(2)}) copy-start(s32[2]{0:T(128)} %param.12) | copy-start | bytes 28
  5.3 220.7 %collective-permute-start.3 = (bf16[1,512,2048]{2,1,0:T(8,128)(2,1)}, bf16[1,512,2048]{2,1,0:T(8,128)(2,1)}, u32[]{:S(2)}, u32[]{:S(2)}) collective-permute-start(bf16[1,512,2048]{2,1,0:T(8,128)(2,1)} %slice.80), channel_id=1, source_target_pairs={{0,16},{16,0},{1,17},{17,1},{2,18},{18,2},{3,19},{19,3},{4,20},{20... | collective-permute-start | bytes 6291464 | tf_op jit(solution)/shard_map/ppermute | solution.py:26
  8.3 224.1 %collective-permute-start.4 = (bf16[1,384,2048]{2,1,0:T(8,128)(2,1)}, bf16[1,384,2048]{2,1,0:T(8,128)(2,1)}, u32[]{:S(2)}, u32[]{:S(2)}) collective-permute-start(bf16[1,384,2048]{2,1,0:T(8,128)(2,1)} %slice.81), channel_id=1, source_target_pairs={{0,16},{16,0},{1,17},{17,1},{2,18},{18,2},{3,19},{19,3},{4,20},{20... | collective-permute-start | bytes 4718600 | tf_op jit(solution)/shard_map/ppermute | solution.py:26
  8.4 228.3 %collective-permute-start = (bf16[1,2048,1024]{2,1,0:T(8,128)(2,1)}, bf16[1,2048,1024]{2,1,0:T(8,128)(2,1)}, u32[]{:S(2)}, u32[]{:S(2)}) collective-permute-start(bf16[1,2048,1024]{2,1,0:T(8,128)(2,1)} %param.14), channel_id=1, source_target_pairs={{0,16},{16,0},{1,17},{17,1},{2,18},{18,2},{3,19},{19,3},{4,20},{20... | collective-permute-start | bytes 12582920 | tf_op jit(solution)/shard_map/ppermute | solution.py:26
  11.0 10.5 %all-to-all-start = ((bf16[4,2,2048]{2,1,0:T(2,128)(2,1)}), bf16[4,2,2048]{2,1,0:T(2,128)(2,1)S(1)}, u32[]{:S(2)}, u32[]{:S(2)}) async-start(bf16[4,2,2048]{2,1,0:T(2,128)(2,1)} %broadcast_in_dim.25), calls=%async_computation | async-start | bytes 65536 | tf_op jit(solution)/shard_map/all_to_all | solution.py:39
  15.9 185.3 %collective-permute-start.2 = (bf16[1,2048,256]{2,1,0:T(8,128)(2,1)}, bf16[1,2048,256]{2,1,0:T(8,128)(2,1)}, u32[]{:S(2)}, u32[]{:S(2)}) collective-permute-start(bf16[1,2048,256]{2,1,0:T(8,128)(2,1)} %param.16), channel_id=1, source_target_pairs={{0,16},{16,0},{1,17},{17,1},{2,18},{18,2},{3,19},{19,3},{4,20},{20... | collective-permute-start | bytes 3145736 | tf_op jit(solution)/shard_map/ppermute | solution.py:26
  16.4 207.3 %collective-permute-start.1 = (bf16[1,2048,256]{2,1,0:T(8,128)(2,1)}, bf16[1,2048,256]{2,1,0:T(8,128)(2,1)}, u32[]{:S(2)}, u32[]{:S(2)}) collective-permute-start(bf16[1,2048,256]{2,1,0:T(8,128)(2,1)} %param.15), channel_id=1, source_target_pairs={{0,16},{16,0},{1,17},{17,1},{2,18},{18,2},{3,19},{19,3},{4,20},{20... | collective-permute-start | bytes 3145736 | tf_op jit(solution)/shard_map/ppermute | solution.py:26
  22.5 7.2 %all-to-all-start.1 = ((bf16[2,4,2048]{2,0,1:T(2,128)(2,1)}), bf16[2,4,2048]{2,0,1:T(2,128)(2,1)S(1)}, u32[]{:S(2)}, u32[]{:S(2)}) async-start(bf16[2,4,2048]{2,0,1:T(2,128)(2,1)} %multiply_convert_fusion), calls=%async_computation.1 | async-start | bytes 65536 | tf_op jit(solution)/shard_map/all_to_all | solution.py:235
  29.7 194.0 %copy-start.9 = (bf16[1,2048,256]{2,1,0:T(8,128)(2,1)S(1)}, bf16[1,2048,256]{2,1,0:T(8,128)(2,1)}, u32[]{:S(2)}) copy-start(bf16[1,2048,256]{2,1,0:T(8,128)(2,1)} %param.15) | copy-start | bytes 3145732
  201.2 44.1 %collective-permute-start.5 = (bf16[1,128,2048]{2,1,0:T(8,128)(2,1)S(1)}, bf16[1,128,2048]{2,1,0:T(8,128)(2,1)S(1)}, u32[]{:S(2)}, u32[]{:S(2)}) collective-permute-start(bf16[1,128,2048]{2,1,0:T(8,128)(2,1)S(1)} %slice.82), channel_id=1, source_target_pairs={{0,16},{16,0},{1,17},{17,1},{2,18},{18,2},{3,19},{19,3},{4,20},{20... | collective-permute-start | bytes 1572872 | tf_op jit(solution)/shard_map/ppermute | solution.py:26
  204.6 20.7 %copy-start.7 = (bf16[1,2048,256]{2,1,0:T(8,128)(2,1)}, bf16[1,2048,256]{2,1,0:T(8,128)(2,1)S(1)}, u32[]{:S(2)}) copy-start(bf16[1,2048,256]{2,1,0:T(8,128)(2,1)S(1)} %broadcast_select_fusion.3) | copy-start | bytes 3145732
  225.0 1.0 copy-start.8
  226.0 2.8 %copy-start.3 = (bf16[1,1024,2048]{2,1,0:T(8,128)(2,1)S(1)}, bf16[1,1024,2048]{2,1,0:T(8,128)(2,1)}, u32[]{:S(2)}) copy-start(bf16[1,1024,2048]{2,1,0:T(8,128)(2,1)} %param.17) | copy-start | bytes 12582916
  228.8 3.6 %copy-start.1 = (bf16[1,512,2048]{2,1,0:T(8,128)(2,1)}, bf16[1,512,2048]{2,1,0:T(8,128)(2,1)S(1)}, u32[]{:S(2)}) copy-start(bf16[1,512,2048]{2,1,0:T(8,128)(2,1)S(1)} %broadcast_select_fusion.1) | copy-start | bytes 6291460
  232.4 4.3 %copy-start.5 = (bf16[1,2048,1024]{2,1,0:T(8,128)(2,1)S(1)}, bf16[1,2048,1024]{2,1,0:T(8,128)(2,1)}, u32[]{:S(2)}) copy-start(bf16[1,2048,1024]{2,1,0:T(8,128)(2,1)} %param.14) | copy-start | bytes 12582916
  234.7 2.0 copy-start.6
  239.4 2.0 copy-start.4
  242.0 7.3 %all-to-all-start.2 = ((f32[4,2,1536]{2,1,0:T(2,128)}), f32[4,2,1536]{2,1,0:T(2,128)S(1)}, u32[]{:S(2)}, u32[]{:S(2)}) async-start(f32[4,2,1536]{2,1,0:T(2,128)} %reshape.142), calls=%async_computation.2 | async-start | bytes 98304 | tf_op jit(solution)/shard_map/all_to_all | solution.py:44
  249.4 3.5 %copy-start.11 = (bf16[2,256]{1,0:T(2,128)(2,1)}, bf16[2,256]{1,0:T(2,128)(2,1)S(1)}, u32[]{:S(2)}) copy-start(bf16[2,256]{1,0:T(2,128)(2,1)S(1)} %slice.128) | copy-start | bytes 3076
  253.5 7.1 %all-to-all-start.3 = ((bf16[4,2,1024]{2,1,0:T(2,128)(2,1)}), bf16[4,2,1024]{2,1,0:T(2,128)(2,1)S(1)}, u32[]{:S(2)}, u32[]{:S(2)}) async-start(bf16[4,2,1024]{2,1,0:T(2,128)(2,1)} %broadcast_in_dim.29), calls=%async_computation.3 | async-start | bytes 32768 | tf_op jit(solution)/shard_map/all_to_all | solution.py:39
